TPU v7x, 32 devices: a whole 2x2x4 slice. The times are simulated.
32 devices in a mesh: sub: 16 (over z, y, core), strip: 2 (over x).
Axes of the slice: x: 2, y: 2, z: 4, core: 2. Of those that a mesh axis runs over, the one named last changes fastest.
Arguments:
- spectra: bfloat16 [32, 256, 2048], P('sub', 'strip'), may hold values from -6 to 6
- offsets: int32 [32], P('sub'), may hold values from 0 to 1023
Outputs:
- foreground: float32 [1024, 256, 32], P('strip', 'sub')
All inputs are finite; a program needn't handle non-finite values.
Results may differ from a plain program's by a relative error of at most 0.0068.
Values may be sent and summed in bfloat16 or wider, within the bound.
A program may use at most 64 MiB of HBM per device.

v0:
```python
import math
import jax
import jax.numpy as jnp
import numpy as np
from jax import lax
from jax.sharding import PartitionSpec as P

KR = 256
ROWS = 1024
COLS = 256
WIN = 8
BG = 16


def from_behind(value, axis, steps):
    count = lax.axis_size(axis)
    pairs = [(source, (source + steps) % count) for source in range(count)]
    return lax.ppermute(value, axis, pairs)


def extended(shard, sides, width):
    for axis, dim in sides:
        count, length = (lax.axis_size(axis), shard.shape[dim])
        up = [(i, (i + 1) % count) for i in range(count - 1)]
        down = [(j, i) for i, j in up]
        last = lax.slice_in_dim(shard, length - width, length, axis=dim)
        leading = lax.slice_in_dim(shard, 0, width, axis=dim)
        before = lax.ppermute(last, axis, up)
        after = lax.ppermute(leading, axis, down)
        shard = jnp.concatenate([before, shard, after], axis=dim)
    return shard


def column_table(samples, width):
    sample_index = jnp.arange(samples, dtype=jnp.int32)[:, None]
    column_index = jnp.arange(width, dtype=jnp.int32)[None, :]
    phase = jnp.mod(sample_index * column_index, samples).astype(jnp.float32) * (
        2.0 * math.pi / samples
    )
    cosine = jnp.cos(phase) / math.sqrt(samples)
    sine = -jnp.sin(phase) / math.sqrt(samples)
    upper = jnp.concatenate([cosine, sine], axis=1)
    lower = jnp.concatenate([-sine, cosine], axis=1)
    return jnp.concatenate([upper, lower], axis=0).astype(jnp.bfloat16)


def row_table(row_index, samples, image_rows):
    sample_index = jnp.arange(samples, dtype=jnp.int32)[None, :] - samples // 2
    phase = jnp.mod(row_index[:, None] * sample_index, image_rows).astype(jnp.float32) * (
        2.0 * math.pi / image_rows
    )
    scale = 1.0 / math.sqrt(samples)
    return jnp.concatenate([jnp.cos(phase) * scale, jnp.sin(phase) * scale], axis=0).astype(
        jnp.bfloat16
    )


def apply_phase(mixed, offsets, sample_index):
    angle = jnp.mod(offsets[:, None] * (sample_index[None, :] - KR // 2), ROWS).astype(
        jnp.float32
    ) * (2.0 * math.pi / ROWS)
    cosine = jnp.cos(angle)[:, :, None]
    sine = jnp.sin(angle)[:, :, None]
    real_part = mixed[:, :, :COLS]
    imag_part = mixed[:, :, COLS:]
    return jnp.concatenate(
        [real_part * cosine - imag_part * sine, real_part * sine + imag_part * cosine], axis=2
    ).astype(jnp.bfloat16)


def window_mask(block_offset, count):
    target = np.arange(count)[:, None]
    source = np.arange(count)[None, :]
    distance = block_offset * count + source - target
    return ((distance >= 0) & (distance < WIN)).astype(np.float32)


def combine_parts(product, strip_rows):
    product = lax.optimization_barrier(product)
    real_part = product[:, :strip_rows, :COLS] - product[:, strip_rows:, COLS:]
    imag_part = product[:, :strip_rows, COLS:] + product[:, strip_rows:, :COLS]
    return jnp.concatenate([real_part, imag_part], axis=2)


def remove_background(stack):
    frame_count = stack.shape[0]
    series = jnp.transpose(stack, (1, 2, 0))
    source = jnp.arange(frame_count, dtype=jnp.int32)[:, None]
    target = jnp.arange(frame_count, dtype=jnp.int32)[None, :]
    behind = jnp.where(jnp.mod(target - source, frame_count) < BG, 1.0 / BG, 0.0).astype(
        jnp.float32
    )
    weights = jnp.where(source == target, 1.0, 0.0).astype(jnp.float32) - behind
    return jnp.einsum("rcg,gf->rcf", series, weights, precision=lax.Precision.HIGHEST)


def body(spectra, offsets):
    sub_dev = spectra.shape[0]
    strip_rows = ROWS // lax.axis_size("strip")
    local_samples = spectra.shape[1]
    first_row = lax.axis_index("strip") * strip_rows
    own_rows = first_row + jnp.arange(strip_rows, dtype=jnp.int32)
    own_samples = lax.axis_index("strip") * local_samples + jnp.arange(
        local_samples, dtype=jnp.int32
    )
    columns = column_table(spectra.shape[2] // 2, COLS)
    table = row_table(own_rows, KR, ROWS)
    passes = (WIN - 2 + sub_dev) // sub_dev
    shifted_local = apply_phase(
        jnp.einsum("skc,cn->skn", spectra, columns, preferred_element_type=jnp.float32),
        offsets,
        own_samples,
    )
    summed = jnp.einsum(
        "ab,bkn->akn",
        jnp.asarray(window_mask(0, sub_dev)),
        shifted_local.astype(jnp.float32),
        precision=lax.Precision.HIGHEST,
    )
    moving = shifted_local
    for block_offset in range(1, passes + 1):
        moving = from_behind(moving, "sub", -1)
        summed = summed + jnp.einsum(
            "ab,bkn->akn",
            jnp.asarray(window_mask(block_offset, sub_dev)),
            moving.astype(jnp.float32),
            precision=lax.Precision.HIGHEST,
        )
    table_wide = table.astype(jnp.float32)
    product = jnp.einsum(
        "mk,skn->smn",
        table_wide,
        lax.all_gather(summed, "strip", axis=1, tiled=True),
        precision=lax.Precision.HIGHEST,
    )
    frames = combine_parts(product, strip_rows)
    real_part = frames[:, :, :COLS]
    imag_part = frames[:, :, COLS:]
    log_power = jnp.log(1.0 + real_part * real_part + imag_part * imag_part)
    padded = extended(log_power, (("strip", 1),), 1)
    padded = jnp.pad(padded, ((0, 0), (0, 0), (1, 1)))
    total = jnp.zeros_like(log_power)
    for row_step in range(3):
        for col_step in range(3):
            total = total + padded[:, row_step : row_step + strip_rows, col_step : col_step + COLS]
    filtered = total / 9.0
    return remove_background(
        lax.all_to_all(filtered, "sub", split_axis=2, concat_axis=0, tiled=True)
    )


def solution(mesh):
    in_specs = (P("sub", "strip", None), P("sub"))
    out_specs = P("strip", "sub", None)
    return jax.shard_map(body, mesh=mesh, in_specs=in_specs, out_specs=out_specs, check_vma=False)
```

profile of v0, /device:TPU:1, one launch (start us, length us, event | category | flops | bytes accessed | tf_op | source)
XLA Modules:
  0.0 140.7 jit_solution(7064883153234936964)
XLA Ops:
  6.5 0.0 copy-start
  6.5 0.0 all-gather.2.cloned.1.call-start
  6.5 4.0 %fusion.26 = bf16[1024,256]{0,1:T(8,128)(2,1)S(1)} fusion(), kind=kLoop, calls=%fused_computation.51 | loop fusion | flops 4456448 | bytes 524288 | tf_op jit(solution)/shard_map/convert.9
  10.5 4.3 %negate_convert_fusion = (bf16[1024,256]{0,1:T(8,128)(2,1)S(1)}, bf16[1024,256]{0,1:T(8,128)(2,1)S(1)}) fusion(), kind=kLoop, calls=%fused_computation.42 | loop fusion | flops 5242880 | bytes 1048576 | tf_op jit(solution)/shard_map/convert.6
  14.9 0.8 fusion.60
  15.6 0.0 copy-done
  15.6 0.0 copy-start.2
  15.7 0.7 fusion.8
  16.4 0.1 subtract_convert_fusion
  16.5 0.1 collective-permute-start
  16.6 6.6 %collective-permute-done = bf16[2,128,512]{1,2,0:T(8,128)(2,1)S(1)} collective-permute-done((bf16[2,128,512]{1,2,0:T(8,128)(2,1)S(1)}, bf16[2,128,512]{1,2,0:T(8,128)(2,1)S(1)}, u32[]{:S(2)}, u32[]{:S(2)}) %collective-permute-start) | collective-permute-done | bytes 262176 | tf_op jit(solution)/shard_map/ppermute | solution.py:18
  23.2 2.7 %collective-permute-start.1 = (bf16[2,128,512]{1,2,0:T(8,128)(2,1)S(1)}, bf16[2,128,512]{1,2,0:T(8,128)(2,1)S(1)}, u32[]{:S(2)}, u32[]{:S(2)}) collective-permute-start(bf16[2,128,512]{1,2,0:T(8,128)(2,1)S(1)} %collective-permute-done), channel_id=1, source_target_pairs={{0,30},{2,0},{4,2},{6,4},{8,6},{10,8},{12,10},{14,12},{16,14},{18,... | collective-permute-start | bytes 786440 | tf_op jit(solution)/shard_map/ppermute | solution.py:18
  26.0 0.2 copy.11
  26.2 2.9 %collective-permute-done.1 = bf16[2,128,512]{1,2,0:T(8,128)(2,1)S(1)} collective-permute-done((bf16[2,128,512]{1,2,0:T(8,128)(2,1)S(1)}, bf16[2,128,512]{1,2,0:T(8,128)(2,1)S(1)}, u32[]{:S(2)}, u32[]{:S(2)}) %collective-permute-start.1) | collective-permute-done | bytes 262176 | tf_op jit(solution)/shard_map/ppermute | solution.py:18
  29.0 5.4 %collective-permute-start.2 = (bf16[2,128,512]{1,2,0:T(8,128)(2,1)S(1)}, bf16[2,128,512]{1,2,0:T(8,128)(2,1)S(1)}, u32[]{:S(2)}, u32[]{:S(2)}) collective-permute-start(bf16[2,128,512]{1,2,0:T(8,128)(2,1)S(1)} %collective-permute-done.1), channel_id=1, source_target_pairs={{0,30},{2,0},{4,2},{6,4},{8,6},{10,8},{12,10},{14,12},{16,14},{18,... | collective-permute-start | bytes 786440 | tf_op jit(solution)/shard_map/ppermute | solution.py:18
  34.5 0.0 copy-done.2
  34.5 1.0 fusion.74
  35.4 0.2 copy.12
  35.7 0.2 copy.13
  35.9 1.0 fusion.57
  36.8 0.2 copy.14
  37.1 0.2 copy.15
  37.3 0.0 collective-permute-done.2
  37.3 5.7 %collective-permute-start.3 = (bf16[2,128,512]{1,2,0:T(8,128)(2,1)S(1)}, bf16[2,128,512]{1,2,0:T(8,128)(2,1)}, u32[]{:S(2)}, u32[]{:S(2)}) collective-permute-start(bf16[2,128,512]{1,2,0:T(8,128)(2,1)S(1)} %collective-permute-done.2), channel_id=1, source_target_pairs={{0,30},{2,0},{4,2},{6,4},{8,6},{10,8},{12,10},{14,12},{16,14},{18,... | collective-permute-start | bytes 786440 | tf_op jit(solution)/shard_map/ppermute | solution.py:18
  42.9 1.0 fusion.55
  43.9 0.0 copy-start.1
  43.9 0.2 copy.16
  44.2 0.2 copy.17
  44.4 1.8 %fusion.53 = f32[128,512,2]{1,2,0:T(2,128)} fusion(bf16[2,128,512]{2,0,1:T(2,128)(2,1)S(1)} %copy.17), kind=kOutput, calls=%fused_computation.98 | convolution fusion | flops 3145728 | bytes 786432 | tf_op jit(solution)/shard_map/ab,bkn->akn/dot_general | solution.py:123
  46.1 1.2 copy.18
  47.4 0.0 collective-permute-done.3
  47.4 1.1 copy.19
  48.5 0.0 copy-done.1
  48.5 1.8 %fusion.75 = f32[128,512,2]{1,2,0:T(2,128)} fusion(bf16[2,128,512]{2,0,1:T(2,128)(2,1)S(1)} %copy.19, f32[2,2,1]{1,0,2:T(2,128)S(1)} %copy-done.1), kind=kOutput, calls=%fused_computation.120 | convolution fusion | flops 3145728 | bytes 786448 | tf_op jit(solution)/shard_map/ab,bkn->akn/dot_general | solution.py:123
  50.3 2.0 %copy.20 = f32[128,512,2]{0,1,2:T(8,128)} copy(f32[128,512,2]{1,2,0:T(2,128)} %fusion.75) | data formatting | bytes 1048576 | tf_op jit(solution)/shard_map/ab,bkn->akn/dot_general | solution.py:123
  52.3 2.0 %add_bitcast_fusion = f32[2,128,512]{1,2,0:T(8,128)} fusion(f32[128,512,2]{0,1,2:T(8,128)} %copy.20, f32[128,512,2]{0,1,2:T(8,128)S(1)} %copy.18, f32[128,512,2]{0,1,2:T(8,128)S(1)} %copy.16, f32[128,512,2]{0,1,2:T(8,128)S(1)} %copy.12, f32[128,512,2]{0,1,2:T(8,128)S(1)} %copy.14), kind=kLoop, calls=%fused_computation.62 | loop fusion | flops 524288 | bytes 3145728 | tf_op jit(solution)/shard_map/add | solution.py:123
  54.3 0.0 all-gather.2.cloned.1.call-update
  54.3 2.5 %multiply_convert_fusion.2 = (bf16[512,256]{1,0:T(8,128)(2,1)S(1)}, bf16[512,256]{1,0:T(8,128)(2,1)S(1)}) fusion(s32[256]{0:T(256)S(1)} %iota_add_fusion.1, s32[512]{0:T(512)S(1)} %iota_add_fusion), kind=kLoop, calls=%fused_computation.61 | loop fusion | flops 2359296 | bytes 527360 | tf_op jit(solution)/shard_map/convert
  56.9 23.5 %all-gather.2.cloned.1.call-done = f32[2,256,512]{1,2,0:T(8,128)} async-done(((f32[2,128,512]{1,2,0:T(8,128)}), f32[2,256,512]{1,2,0:T(8,128)}) %all-gather.2.cloned.1.call-update) | async-done | bytes 1048592 | tf_op jit(solution)/shard_map/all_gather | solution.py:133
  80.4 3.1 %convolution_bitcast_fusion = f32[2,1024,512]{1,2,0:T(8,128)S(1)} fusion(f32[2,256,512]{1,2,0:T(8,128)} %all-gather.2.cloned.1.call-done, bf16[512,256]{1,0:T(8,128)(2,1)S(1)} %get-tuple-element.10, bf16[512,256]{1,0:T(8,128)(2,1)S(1)} %get-tuple-element.9), kind=kOutput, calls=%fused_computation | convolution fusion | flops 3222274048 | bytes 5767168 | tf_op jit(solution)/shard_map/mk,skn->smn/dot_general | solution.py:130
  83.5 0.5 fusion.18
  84.0 0.1 fusion.73
  84.1 2.2 %collective-permute-start.4 = (f32[2,1,256]{1,2,0:T(8,128)S(1)}, f32[2,1,256]{1,2,0:T(8,128)S(1)}, u32[]{:S(2)}, u32[]{:S(2)}) collective-permute-start(f32[2,1,256]{1,2,0:T(8,128)S(1)} %get-tuple-element.5), channel_id=1, source_target_pairs={{0,1},{2,3},{4,5},{6,7},{8,9},{10,11},{12,13},{14,15},{16,17},{18,... | collective-permute-start | bytes 6152 | tf_op jit(solution)/shard_map/ppermute | solution.py:28
  86.3 1.3 collective-permute-start.5
  87.6 3.7 %collective-permute-done.4 = f32[2,1,256]{1,2,0:T(8,128)S(1)} collective-permute-done((f32[2,1,256]{1,2,0:T(8,128)S(1)}, f32[2,1,256]{1,2,0:T(8,128)S(1)}, u32[]{:S(2)}, u32[]{:S(2)}) %collective-permute-start.4) | collective-permute-done | bytes 2080 | tf_op jit(solution)/shard_map/ppermute | solution.py:28
  91.3 3.8 %collective-permute-done.5 = f32[2,1,256]{1,2,0:T(8,128)S(1)} collective-permute-done((f32[2,1,256]{1,2,0:T(8,128)S(1)}, f32[2,1,256]{1,2,0:T(8,128)S(1)}, u32[]{:S(2)}, u32[]{:S(2)}) %collective-permute-start.5) | collective-permute-done | bytes 2080 | tf_op jit(solution)/shard_map/ppermute | solution.py:29
  95.1 0.5 select_maximum_fusion
  95.6 1.8 %fusion.12 = f32[2,512,256]{1,2,0:T(8,128)S(1)} fusion(f32[2,514,258]{1,2,0:T(8,128)S(1)} %select_maximum_fusion, f32[2,1,256]{1,2,0:T(8,128)S(1)} %collective-permute-done.5, f32[2,512,256]{1,2,0:T(8,128)S(1)} %fusion.18, f32[2,1,256]{1,2,0:T(8,128)S(1)} %collective-permute-done.4), kind=kLoop, calls=%fused_computation.22 | loop fusion | flops 2883584 | bytes 8392704 | tf_op jit(solution)/shard_map/div | solution.py:146
  97.4 0.8 copy.9
  98.2 32.4 %all_to_all.18 = f32[2,512,256]{1,0,2:T(2,128)S(1)} all-to-all(f32[2,512,256]{1,0,2:T(2,128)S(1)} %copy.9), channel_id=1, replica_groups=mesh['sub'=16,'strip'=2] {'sub'}, dimensions={2} | all-to-all | bytes 2097152 | tf_op jit(solution)/shard_map/all_to_all | solution.py:148
  130.6 0.5 copy.22
  131.2 0.7 all_to_all.16
  131.9 2.0 %fusion.21 = f32[512,16,32]{0,2,1:T(8,128)} fusion(f32[32,512,16]{1,0,2:T(8,128)S(1)} %all_to_all.16), kind=kOutput, calls=%fused_computation.39 | convolution fusion | flops 100680704 | bytes 2097152 | tf_op jit(solution)/shard_map/rcg,gf->rcf/dot_general | solution.py:94
  (4 shorter events, 0.0 us)
Async XLA Ops:
  6.5 9.1 %copy-start = (bf16[2,128,2048]{2,1,0:T(8,128)(2,1)S(1)}, bf16[2,128,2048]{2,1,0:T(8,128)(2,1)}, u32[]{:S(2)}) copy-start(bf16[2,128,2048]{2,1,0:T(8,128)(2,1)} %param.7) | copy-start | bytes 3145732
  6.5 73.8 %all-gather.2.cloned.1.call-start = ((), (), s32[]{:S(2)}) async-start(), calls=%async_computation.1 | async-start | bytes 1572864 | tf_op jit(solution)/shard_map/all_gather | solution.py:133
  15.6 18.8 %copy-start.2 = (f32[2,2,1]{1,0,2:T(2,128)S(1)}, f32[2,2,1]{1,0,2:T(2,128)}, u32[]{:S(2)}) copy-start(f32[2,2,1]{1,0,2:T(2,128)} %constant.94) | copy-start | bytes 52
  16.5 6.7 %collective-permute-start = (bf16[2,128,512]{1,2,0:T(8,128)(2,1)S(1)}, bf16[2,128,512]{1,2,0:T(8,128)(2,1)S(1)}, u32[]{:S(2)}, u32[]{:S(2)}) collective-permute-start(bf16[2,128,512]{1,2,0:T(8,128)(2,1)S(1)} %pad_maximum_fusion.2), channel_id=1, source_target_pairs={{0,30},{2,0},{4,2},{6,4},{8,6},{10,8},{12,10},{14,12},{16,14},{18,... | collective-permute-start | bytes 786440 | tf_op jit(solution)/shard_map/ppermute | solution.py:18
  23.2 5.8 %collective-permute-start.1 = (bf16[2,128,512]{1,2,0:T(8,128)(2,1)S(1)}, bf16[2,128,512]{1,2,0:T(8,128)(2,1)S(1)}, u32[]{:S(2)}, u32[]{:S(2)}) collective-permute-start(bf16[2,128,512]{1,2,0:T(8,128)(2,1)S(1)} %collective-permute-done), channel_id=1, source_target_pairs={{0,30},{2,0},{4,2},{6,4},{8,6},{10,8},{12,10},{14,12},{16,14},{18,... | collective-permute-start | bytes 786440 | tf_op jit(solution)/shard_map/ppermute | solution.py:18
  29.0 8.2 %collective-permute-start.2 = (bf16[2,128,512]{1,2,0:T(8,128)(2,1)S(1)}, bf16[2,128,512]{1,2,0:T(8,128)(2,1)S(1)}, u32[]{:S(2)}, u32[]{:S(2)}) collective-permute-start(bf16[2,128,512]{1,2,0:T(8,128)(2,1)S(1)} %collective-permute-done.1), channel_id=1, source_target_pairs={{0,30},{2,0},{4,2},{6,4},{8,6},{10,8},{12,10},{14,12},{16,14},{18,... | collective-permute-start | bytes 786440 | tf_op jit(solution)/shard_map/ppermute | solution.py:18
  37.3 10.1 %collective-permute-start.3 = (bf16[2,128,512]{1,2,0:T(8,128)(2,1)S(1)}, bf16[2,128,512]{1,2,0:T(8,128)(2,1)}, u32[]{:S(2)}, u32[]{:S(2)}) collective-permute-start(bf16[2,128,512]{1,2,0:T(8,128)(2,1)S(1)} %collective-permute-done.2), channel_id=1, source_target_pairs={{0,30},{2,0},{4,2},{6,4},{8,6},{10,8},{12,10},{14,12},{16,14},{18,... | collective-permute-start | bytes 786440 | tf_op jit(solution)/shard_map/ppermute | solution.py:18
  43.9 4.6 %copy-start.1 = (f32[2,2,1]{1,0,2:T(2,128)S(1)}, f32[2,2,1]{1,0,2:T(2,128)}, u32[]{:S(2)}) copy-start(f32[2,2,1]{1,0,2:T(2,128)} %constant.95) | copy-start | bytes 52
  84.1 7.2 %collective-permute-start.4 = (f32[2,1,256]{1,2,0:T(8,128)S(1)}, f32[2,1,256]{1,2,0:T(8,128)S(1)}, u32[]{:S(2)}, u32[]{:S(2)}) collective-permute-start(f32[2,1,256]{1,2,0:T(8,128)S(1)} %get-tuple-element.5), channel_id=1, source_target_pairs={{0,1},{2,3},{4,5},{6,7},{8,9},{10,11},{12,13},{14,15},{16,17},{18,... | collective-permute-start | bytes 6152 | tf_op jit(solution)/shard_map/ppermute | solution.py:28
  86.3 8.8 %collective-permute-start.5 = (f32[2,1,256]{1,2,0:T(8,128)S(1)}, f32[2,1,256]{1,2,0:T(8,128)S(1)}, u32[]{:S(2)}, u32[]{:S(2)}) collective-permute-start(f32[2,1,256]{1,2,0:T(8,128)S(1)} %get-tuple-element.6), channel_id=1, source_target_pairs={{1,0},{3,2},{5,4},{7,6},{9,8},{11,10},{13,12},{15,14},{17,16},{19,... | collective-permute-start | bytes 6152 | tf_op jit(solution)/shard_map/ppermute | solution.py:29
Sparse Core Ops, SparseCore 0:
  54.4 25.8 all-gather.1
where the time goes:
time: 141 us
  waiting for transfers between devices  40.6 us (29%)
  blocking collectives  32.4 us (23%)
  starting transfers between devices  17.3 us (12%)
  other arithmetic  16.4 us (12%)
  between operations  13.7 us (10%)
  matrix products  12.3 us (9%)
  local copies, waits for them, and re-layouts  8.09 us (6%)
    all_to_all x1, blocking collectives, body(): lax.all_to_all(filtered, 'sub', split_axis=2, concat_axis=0, tiled=True)  32.4 us
    all_gather x1, waiting for transfers between devices, body(): lax.all_gather(summed, 'strip', axis=1, tiled=True)  23.5 us
    ppermute x4, starting transfers between devices, from_behind(): return lax.ppermute(value, axis, pairs)  13.9 us
    another operation x4, other arithmetic  10.9 us
    ppermute x4, waiting for transfers between devices, from_behind(): return lax.ppermute(value, axis, pairs)  9.54 us
    dot_general x4, matrix products, body(): jnp.einsum('ab,bkn->akn', jnp.asarray(window_mask(block_offset, sub_dev))...  5.45 us
    ppermute x1, waiting for transfers between devices, extended(): after = lax.ppermute(leading, axis, down)  3.85 us
    dot_general x4, local copies, waits for them, and re-layouts, body(): jnp.einsum('ab,bkn->akn', jnp.asarray(window_mask(block_offset, sub_dev))...  3.73 us
  transfers between devices with their start and end apart: 7, of which 5 were waited for; matrix products, arithmetic and copies ran while one was open for 7% of the time, Pallas kernels for 0%

commit v1 on v0

--- a/solution.py
+++ b/solution.py
@@ -145,7 +145,12 @@
             total = total + padded[:, row_step : row_step + strip_rows, col_step : col_step + COLS]
     filtered = total / 9.0
     return remove_background(
-        lax.all_to_all(filtered, "sub", split_axis=2, concat_axis=0, tiled=True)
+        jnp.concatenate(
+            lax.all_to_all(
+                jnp.stack(jnp.split(filtered, lax.axis_size("sub"), axis=2)), "sub", 0, 0
+            ),
+            axis=0,
+        )
     )
 
 

time: 141 us -> 140 us (level)
  local copies, waits for them, and re-layouts: 8.09 us -> 6.13 us
where the time goes in v1:
time: 140 us
  waiting for transfers between devices  40.6 us (29%)
  blocking collectives  32.4 us (23%)
  starting transfers between devices  17.3 us (12%)
  other arithmetic  16.4 us (12%)
  between operations  13.8 us (10%)
  matrix products  12.9 us (9%)
  local copies, waits for them, and re-layouts  6.13 us (4%)
    all_to_all x1, blocking collectives, body(): lax.all_to_all(jnp.stack(jnp.split(filtered, lax.axis_size('sub'), axis=2...  32.4 us
    all_gather x1, waiting for transfers between devices, body(): lax.all_gather(summed, 'strip', axis=1, tiled=True)  23.5 us
    ppermute x4, starting transfers between devices, from_behind(): return lax.ppermute(value, axis, pairs)  13.9 us
    another operation x4, other arithmetic  10.9 us
    ppermute x4, waiting for transfers between devices, from_behind(): return lax.ppermute(value, axis, pairs)  9.54 us
    dot_general x4, matrix products, body(): jnp.einsum('ab,bkn->akn', jnp.asarray(window_mask(block_offset, sub_dev))...  5.45 us
    ppermute x1, waiting for transfers between devices, extended(): after = lax.ppermute(leading, axis, down)  3.85 us
    dot_general x4, local copies, waits for them, and re-layouts, body(): jnp.einsum('ab,bkn->akn', jnp.asarray(window_mask(block_offset, sub_dev))...  3.73 us
  transfers between devices with their start and end apart: 7, of which 5 were waited for; matrix products, arithmetic and copies ran while one was open for 7% of the time, Pallas kernels for 0%

profile of v1, /device:TPU:1, one launch (start us, length us, event | category | flops | bytes accessed | tf_op | source)
XLA Modules:
  0.0 139.5 jit_solution(18002861768679792401)
XLA Ops:
  6.5 0.0 copy-start
  6.5 0.0 all-gather.2.cloned.1.call-start
  6.5 4.0 %fusion.27 = bf16[1024,256]{0,1:T(8,128)(2,1)S(1)} fusion(), kind=kLoop, calls=%fused_computation.51 | loop fusion | flops 4456448 | bytes 524288 | tf_op jit(solution)/shard_map/convert.9
  10.5 4.3 %negate_convert_fusion = (bf16[1024,256]{0,1:T(8,128)(2,1)S(1)}, bf16[1024,256]{0,1:T(8,128)(2,1)S(1)}) fusion(), kind=kLoop, calls=%fused_computation.42 | loop fusion | flops 5242880 | bytes 1048576 | tf_op jit(solution)/shard_map/convert.6
  14.9 0.8 fusion.77
  15.6 0.0 copy-done
  15.6 0.0 copy-start.2
  15.7 0.7 fusion.8
  16.4 0.1 subtract_convert_fusion
  16.5 0.1 collective-permute-start
  16.6 6.6 %collective-permute-done = bf16[2,128,512]{1,2,0:T(8,128)(2,1)S(1)} collective-permute-done((bf16[2,128,512]{1,2,0:T(8,128)(2,1)S(1)}, bf16[2,128,512]{1,2,0:T(8,128)(2,1)S(1)}, u32[]{:S(2)}, u32[]{:S(2)}) %collective-permute-start) | collective-permute-done | bytes 262176 | tf_op jit(solution)/shard_map/ppermute | solution.py:18
  23.2 2.7 %collective-permute-start.1 = (bf16[2,128,512]{1,2,0:T(8,128)(2,1)S(1)}, bf16[2,128,512]{1,2,0:T(8,128)(2,1)S(1)}, u32[]{:S(2)}, u32[]{:S(2)}) collective-permute-start(bf16[2,128,512]{1,2,0:T(8,128)(2,1)S(1)} %collective-permute-done), channel_id=1, source_target_pairs={{0,30},{2,0},{4,2},{6,4},{8,6},{10,8},{12,10},{14,12},{16,14},{18,... | collective-permute-start | bytes 786440 | tf_op jit(solution)/shard_map/ppermute | solution.py:18
  26.0 0.2 copy.9
  26.2 2.9 %collective-permute-done.1 = bf16[2,128,512]{1,2,0:T(8,128)(2,1)S(1)} collective-permute-done((bf16[2,128,512]{1,2,0:T(8,128)(2,1)S(1)}, bf16[2,128,512]{1,2,0:T(8,128)(2,1)S(1)}, u32[]{:S(2)}, u32[]{:S(2)}) %collective-permute-start.1) | collective-permute-done | bytes 262176 | tf_op jit(solution)/shard_map/ppermute | solution.py:18
  29.0 5.4 %collective-permute-start.2 = (bf16[2,128,512]{1,2,0:T(8,128)(2,1)S(1)}, bf16[2,128,512]{1,2,0:T(8,128)(2,1)S(1)}, u32[]{:S(2)}, u32[]{:S(2)}) collective-permute-start(bf16[2,128,512]{1,2,0:T(8,128)(2,1)S(1)} %collective-permute-done.1), channel_id=1, source_target_pairs={{0,30},{2,0},{4,2},{6,4},{8,6},{10,8},{12,10},{14,12},{16,14},{18,... | collective-permute-start | bytes 786440 | tf_op jit(solution)/shard_map/ppermute | solution.py:18
  34.5 0.0 copy-done.2
  34.5 1.0 fusion.91
  35.4 0.2 copy.10
  35.7 0.2 copy.11
  35.9 1.0 fusion.74
  36.8 0.2 copy.12
  37.1 0.2 copy.13
  37.3 0.0 collective-permute-done.2
  37.3 5.7 %collective-permute-start.3 = (bf16[2,128,512]{1,2,0:T(8,128)(2,1)S(1)}, bf16[2,128,512]{1,2,0:T(8,128)(2,1)}, u32[]{:S(2)}, u32[]{:S(2)}) collective-permute-start(bf16[2,128,512]{1,2,0:T(8,128)(2,1)S(1)} %collective-permute-done.2), channel_id=1, source_target_pairs={{0,30},{2,0},{4,2},{6,4},{8,6},{10,8},{12,10},{14,12},{16,14},{18,... | collective-permute-start | bytes 786440 | tf_op jit(solution)/shard_map/ppermute | solution.py:18
  42.9 1.0 fusion.72
  43.9 0.0 copy-start.1
  43.9 0.2 copy.14
  44.2 0.2 copy.15
  44.4 1.8 %fusion.70 = f32[128,512,2]{1,2,0:T(2,128)} fusion(bf16[2,128,512]{2,0,1:T(2,128)(2,1)S(1)} %copy.15), kind=kOutput, calls=%fused_computation.130 | convolution fusion | flops 3145728 | bytes 786432 | tf_op jit(solution)/shard_map/ab,bkn->akn/dot_general | solution.py:123
  46.1 1.2 copy.16
  47.4 0.0 collective-permute-done.3
  47.4 1.1 copy.17
  48.5 0.0 copy-done.1
  48.5 1.8 %fusion.92 = f32[128,512,2]{1,2,0:T(2,128)} fusion(bf16[2,128,512]{2,0,1:T(2,128)(2,1)S(1)} %copy.17, f32[2,2,1]{1,0,2:T(2,128)S(1)} %copy-done.1), kind=kOutput, calls=%fused_computation.152 | convolution fusion | flops 3145728 | bytes 786448 | tf_op jit(solution)/shard_map/ab,bkn->akn/dot_general | solution.py:123
  50.3 2.0 %copy.18 = f32[128,512,2]{0,1,2:T(8,128)} copy(f32[128,512,2]{1,2,0:T(2,128)} %fusion.92) | data formatting | bytes 1048576 | tf_op jit(solution)/shard_map/ab,bkn->akn/dot_general | solution.py:123
  52.3 2.0 %add_bitcast_fusion = f32[2,128,512]{1,2,0:T(8,128)} fusion(f32[128,512,2]{0,1,2:T(8,128)} %copy.18, f32[128,512,2]{0,1,2:T(8,128)S(1)} %copy.16, f32[128,512,2]{0,1,2:T(8,128)S(1)} %copy.14, f32[128,512,2]{0,1,2:T(8,128)S(1)} %copy.10, f32[128,512,2]{0,1,2:T(8,128)S(1)} %copy.12), kind=kLoop, calls=%fused_computation.62 | loop fusion | flops 524288 | bytes 3145728 | tf_op jit(solution)/shard_map/add | solution.py:123
  54.3 0.0 all-gather.2.cloned.1.call-update
  54.3 2.5 %multiply_convert_fusion.2 = (bf16[512,256]{1,0:T(8,128)(2,1)S(1)}, bf16[512,256]{1,0:T(8,128)(2,1)S(1)}) fusion(s32[256]{0:T(256)S(1)} %iota_add_fusion.1, s32[512]{0:T(512)S(1)} %iota_add_fusion), kind=kLoop, calls=%fused_computation.61 | loop fusion | flops 2359296 | bytes 527360 | tf_op jit(solution)/shard_map/convert
  56.9 23.5 %all-gather.2.cloned.1.call-done = f32[2,256,512]{1,2,0:T(8,128)} async-done(((f32[2,128,512]{1,2,0:T(8,128)}), f32[2,256,512]{1,2,0:T(8,128)}) %all-gather.2.cloned.1.call-update) | async-done | bytes 1048592 | tf_op jit(solution)/shard_map/all_gather | solution.py:133
  80.4 3.1 %convolution_bitcast_fusion = f32[2,1024,512]{1,2,0:T(8,128)S(1)} fusion(f32[2,256,512]{1,2,0:T(8,128)} %all-gather.2.cloned.1.call-done, bf16[512,256]{1,0:T(8,128)(2,1)S(1)} %get-tuple-element.10, bf16[512,256]{1,0:T(8,128)(2,1)S(1)} %get-tuple-element.9), kind=kOutput, calls=%fused_computation | convolution fusion | flops 3222274048 | bytes 5767168 | tf_op jit(solution)/shard_map/mk,skn->smn/dot_general | solution.py:130
  83.5 0.5 fusion.18
  84.0 0.1 fusion.90
  84.1 2.2 %collective-permute-start.4 = (f32[2,1,256]{1,2,0:T(8,128)S(1)}, f32[2,1,256]{1,2,0:T(8,128)S(1)}, u32[]{:S(2)}, u32[]{:S(2)}) collective-permute-start(f32[2,1,256]{1,2,0:T(8,128)S(1)} %get-tuple-element.5), channel_id=1, source_target_pairs={{0,1},{2,3},{4,5},{6,7},{8,9},{10,11},{12,13},{14,15},{16,17},{18,... | collective-permute-start | bytes 6152 | tf_op jit(solution)/shard_map/ppermute | solution.py:28
  86.3 1.3 collective-permute-start.5
  87.6 3.7 %collective-permute-done.4 = f32[2,1,256]{1,2,0:T(8,128)S(1)} collective-permute-done((f32[2,1,256]{1,2,0:T(8,128)S(1)}, f32[2,1,256]{1,2,0:T(8,128)S(1)}, u32[]{:S(2)}, u32[]{:S(2)}) %collective-permute-start.4) | collective-permute-done | bytes 2080 | tf_op jit(solution)/shard_map/ppermute | solution.py:28
  91.3 3.8 %collective-permute-done.5 = f32[2,1,256]{1,2,0:T(8,128)S(1)} collective-permute-done((f32[2,1,256]{1,2,0:T(8,128)S(1)}, f32[2,1,256]{1,2,0:T(8,128)S(1)}, u32[]{:S(2)}, u32[]{:S(2)}) %collective-permute-start.5) | collective-permute-done | bytes 2080 | tf_op jit(solution)/shard_map/ppermute | solution.py:29
  95.1 0.5 select_maximum_fusion
  95.6 1.8 %fusion.12 = f32[2,512,256]{1,2,0:T(8,128)S(1)} fusion(f32[2,514,258]{1,2,0:T(8,128)S(1)} %select_maximum_fusion, f32[2,1,256]{1,2,0:T(8,128)S(1)} %collective-permute-done.5, f32[2,512,256]{1,2,0:T(8,128)S(1)} %fusion.18, f32[2,1,256]{1,2,0:T(8,128)S(1)} %collective-permute-done.4), kind=kLoop, calls=%fused_computation.22 | loop fusion | flops 2883584 | bytes 8392704 | tf_op jit(solution)/shard_map/div | solution.py:146
  97.7 32.4 %all_to_all.5 = f32[16,2,512,16]{2,3,1,0:T(8,128)S(1)} all-to-all(f32[16,2,512,16]{2,3,1,0:T(8,128)S(1)} %fusion.33), channel_id=1, replica_groups=mesh['sub'=16,'strip'=2] {'sub'}, dimensions={0} | all-to-all | bytes 2097152 | tf_op jit(solution)/shard_map/all_to_all | solution.py:149
  130.0 2.7 %fusion.21 = f32[512,16,32]{0,2,1:T(8,128)} fusion(f32[32,512,16]{1,2,0:T(8,128)S(1)} %bitcast.96), kind=kOutput, calls=%fused_computation.39 | convolution fusion | flops 100680704 | bytes 2097152 | tf_op jit(solution)/shard_map/rcg,gf->rcf/dot_general | solution.py:94
  (20 shorter events, 0.1 us)
Async XLA Ops:
  6.5 9.1 %copy-start = (bf16[2,128,2048]{2,1,0:T(8,128)(2,1)S(1)}, bf16[2,128,2048]{2,1,0:T(8,128)(2,1)}, u32[]{:S(2)}) copy-start(bf16[2,128,2048]{2,1,0:T(8,128)(2,1)} %param.7) | copy-start | bytes 3145732
  6.5 73.8 %all-gather.2.cloned.1.call-start = ((), (), s32[]{:S(2)}) async-start(), calls=%async_computation.1 | async-start | bytes 1572864 | tf_op jit(solution)/shard_map/all_gather | solution.py:133
  15.6 18.8 %copy-start.2 = (f32[2,2,1]{1,0,2:T(2,128)S(1)}, f32[2,2,1]{1,0,2:T(2,128)}, u32[]{:S(2)}) copy-start(f32[2,2,1]{1,0,2:T(2,128)} %constant.94) | copy-start | bytes 52
  16.5 6.7 %collective-permute-start = (bf16[2,128,512]{1,2,0:T(8,128)(2,1)S(1)}, bf16[2,128,512]{1,2,0:T(8,128)(2,1)S(1)}, u32[]{:S(2)}, u32[]{:S(2)}) collective-permute-start(bf16[2,128,512]{1,2,0:T(8,128)(2,1)S(1)} %pad_maximum_fusion.2), channel_id=1, source_target_pairs={{0,30},{2,0},{4,2},{6,4},{8,6},{10,8},{12,10},{14,12},{16,14},{18,... | collective-permute-start | bytes 786440 | tf_op jit(solution)/shard_map/ppermute | solution.py:18
  23.2 5.8 %collective-permute-start.1 = (bf16[2,128,512]{1,2,0:T(8,128)(2,1)S(1)}, bf16[2,128,512]{1,2,0:T(8,128)(2,1)S(1)}, u32[]{:S(2)}, u32[]{:S(2)}) collective-permute-start(bf16[2,128,512]{1,2,0:T(8,128)(2,1)S(1)} %collective-permute-done), channel_id=1, source_target_pairs={{0,30},{2,0},{4,2},{6,4},{8,6},{10,8},{12,10},{14,12},{16,14},{18,... | collective-permute-start | bytes 786440 | tf_op jit(solution)/shard_map/ppermute | solution.py:18
  29.0 8.2 %collective-permute-start.2 = (bf16[2,128,512]{1,2,0:T(8,128)(2,1)S(1)}, bf16[2,128,512]{1,2,0:T(8,128)(2,1)S(1)}, u32[]{:S(2)}, u32[]{:S(2)}) collective-permute-start(bf16[2,128,512]{1,2,0:T(8,128)(2,1)S(1)} %collective-permute-done.1), channel_id=1, source_target_pairs={{0,30},{2,0},{4,2},{6,4},{8,6},{10,8},{12,10},{14,12},{16,14},{18,... | collective-permute-start | bytes 786440 | tf_op jit(solution)/shard_map/ppermute | solution.py:18
  37.3 10.1 %collective-permute-start.3 = (bf16[2,128,512]{1,2,0:T(8,128)(2,1)S(1)}, bf16[2,128,512]{1,2,0:T(8,128)(2,1)}, u32[]{:S(2)}, u32[]{:S(2)}) collective-permute-start(bf16[2,128,512]{1,2,0:T(8,128)(2,1)S(1)} %collective-permute-done.2), channel_id=1, source_target_pairs={{0,30},{2,0},{4,2},{6,4},{8,6},{10,8},{12,10},{14,12},{16,14},{18,... | collective-permute-start | bytes 786440 | tf_op jit(solution)/shard_map/ppermute | solution.py:18
  43.9 4.6 %copy-start.1 = (f32[2,2,1]{1,0,2:T(2,128)S(1)}, f32[2,2,1]{1,0,2:T(2,128)}, u32[]{:S(2)}) copy-start(f32[2,2,1]{1,0,2:T(2,128)} %constant.95) | copy-start | bytes 52
  84.1 7.2 %collective-permute-start.4 = (f32[2,1,256]{1,2,0:T(8,128)S(1)}, f32[2,1,256]{1,2,0:T(8,128)S(1)}, u32[]{:S(2)}, u32[]{:S(2)}) collective-permute-start(f32[2,1,256]{1,2,0:T(8,128)S(1)} %get-tuple-element.5), channel_id=1, source_target_pairs={{0,1},{2,3},{4,5},{6,7},{8,9},{10,11},{12,13},{14,15},{16,17},{18,... | collective-permute-start | bytes 6152 | tf_op jit(solution)/shard_map/ppermute | solution.py:28
  86.3 8.8 %collective-permute-start.5 = (f32[2,1,256]{1,2,0:T(8,128)S(1)}, f32[2,1,256]{1,2,0:T(8,128)S(1)}, u32[]{:S(2)}, u32[]{:S(2)}) collective-permute-start(f32[2,1,256]{1,2,0:T(8,128)S(1)} %get-tuple-element.6), channel_id=1, source_target_pairs={{1,0},{3,2},{5,4},{7,6},{9,8},{11,10},{13,12},{15,14},{17,16},{19,... | collective-permute-start | bytes 6152 | tf_op jit(solution)/shard_map/ppermute | solution.py:29
Sparse Core Ops, SparseCore 0:
  54.4 25.8 all-gather.1
